TPU v7x, 32 devices: a whole 2x2x4 slice. The times are simulated.
32 devices in a mesh: gx: 8 (over z, y), gy: 2 (over core), gz: 2 (over x).
Axes of the slice: x: 2, y: 2, z: 4, core: 2. Of those that a mesh axis runs over, the one named last changes fastest.
Arguments:
- populations: float32 [39, 24, 8, 256], P(None, 'gx', 'gy', 'gz'), may hold values from 0.5 to 1.5
- pore_mask: int32 [24, 8, 256], P('gx', 'gy', 'gz'), may hold values 0 or 1
Outputs:
- advanced: float32 [39, 24, 8, 256], P(None, 'gx', 'gy', 'gz')
All inputs are finite; a program needn't handle non-finite values. No bound on the sum of `pore_mask` on one device may be relied on, other than what follows from the above.
Results may differ from a plain program's by a relative error of at most 0.0003.
Values sent between devices are 32-bit elements; how exact they have to be, the bound alone decides.
A program may use at most 64 MiB of HBM per device.

v0:
```python
import jax
import jax.numpy as jnp
from jax import lax
from jax.sharding import PartitionSpec as P

sound_sq = 2.0 / 3.0
relax_time = 0.8
pair_list = [(0, 0), (1, 1), (2, 2), (0, 1), (0, 2), (1, 2)]
triple_list = [
    (0, 0, 0),
    (1, 1, 1),
    (2, 2, 2),
    (0, 0, 1),
    (0, 0, 2),
    (1, 1, 0),
    (1, 1, 2),
    (2, 2, 0),
    (2, 2, 1),
    (0, 1, 2),
]


def extended(cells, sides, width):
    for axis, dim in sides:
        count = lax.axis_size(axis)
        head = lax.slice_in_dim(cells, 0, width, axis=dim)
        tail = lax.slice_in_dim(cells, cells.shape[dim] - width, cells.shape[dim], axis=dim)
        cells = jnp.concatenate(
            [
                lax.ppermute(tail, axis, [(i, (i + 1) % count) for i in range(count)]),
                cells,
                lax.ppermute(head, axis, [((i + 1) % count, i) for i in range(count)]),
            ],
            axis=dim,
        )
    return cells


def lattice_tables():
    shell_weights = {
        (0, 0, 0): 1.0 / 12.0,
        (0, 0, 1): 1.0 / 12.0,
        (1, 1, 1): 1.0 / 27.0,
        (0, 0, 2): 2.0 / 135.0,
        (0, 2, 2): 1.0 / 432.0,
        (0, 0, 3): 1.0 / 1620.0,
    }
    speed_list = []
    weight_list = []
    for a in range(-3, 4):
        for b in range(-3, 4):
            for c in range(-3, 4):
                pattern = tuple(sorted((abs(a), abs(b), abs(c))))
                if pattern in shell_weights:
                    speed_list.append((a, b, c))
                    weight_list.append(shell_weights[pattern])
    count = len(speed_list)
    opposite = [speed_list.index((-v[0], -v[1], -v[2])) for v in speed_list]
    hermite = [[1.0] * count]
    scaling = [1.0]
    for a in range(3):
        hermite.append([float(v[a]) for v in speed_list])
        scaling.append(1.0 / sound_sq)
    for a, b in pair_list:
        hermite.append([float(v[a] * v[b]) - sound_sq * float(a == b) for v in speed_list])
        scaling.append((1.0 if a == b else 2.0) / (2.0 * sound_sq**2))
    for a, b, c in triple_list:
        hermite.append(
            [
                float(v[a] * v[b] * v[c])
                - sound_sq * (v[a] * float(b == c) + v[b] * float(a == c) + v[c] * float(a == b))
                for v in speed_list
            ]
        )
        distinct = len(set((a, b, c)))
        scaling.append({1: 1.0, 2: 3.0, 3: 6.0}[distinct] / (6.0 * sound_sq**3))
    moment_count = len(hermite)
    project = [[hermite[j][k] * weight_list[k] for k in range(count)] for j in range(moment_count)]
    gram_matrix = [
        [sum((project[i][k] * hermite[j][k] for k in range(count))) for j in range(moment_count)]
        for i in range(moment_count)
    ]
    hermite_t = [[hermite[j][k] for j in range(moment_count)] for k in range(count)]
    relaxing = [
        (1.0 - 1.0 / relax_time) * scaling[j] if j >= 4 else 0.0 for j in range(moment_count)
    ]
    return (
        jnp.asarray(hermite_t, dtype=jnp.float32),
        jnp.asarray(project, dtype=jnp.float32),
        jnp.asarray(gram_matrix, dtype=jnp.float32),
        jnp.asarray(scaling, dtype=jnp.float32),
        jnp.asarray(relaxing, dtype=jnp.float32),
        speed_list,
        opposite,
    )


def collide(state, pore_mask, tables):
    hermite_t, project, gram_matrix, scaling, relaxing, speeds, opposite = tables
    pop_count = state.shape[0]
    columns = state.reshape(pop_count, -1)
    moments = jnp.dot(project, columns, precision=lax.Precision.HIGHEST)
    density = moments[0]
    velocity = [moments[1 + a] / density for a in range(3)]
    pieces_list = [density] + [density * velocity[a] for a in range(3)]
    pieces_list = pieces_list + [density * velocity[a] * velocity[b] for a, b in pair_list]
    pieces_list = pieces_list + [
        density * velocity[a] * velocity[b] * velocity[c] for a, b, c in triple_list
    ]
    equilibrium = scaling[:, None] * jnp.stack(pieces_list)
    excess = moments - jnp.dot(gram_matrix, equilibrium, precision=lax.Precision.HIGHEST)
    coeffs = equilibrium + relaxing[:, None] * excess
    collided = jnp.dot(hermite_t, coeffs, precision=lax.Precision.HIGHEST)
    mirrored = jnp.stack([columns[opposite[k]] for k in range(pop_count)])
    return jnp.where(pore_mask.reshape(1, -1) == 1, collided, mirrored).reshape(state.shape)


def stream(padded, speeds):
    extent_x = padded.shape[1] - 6
    extent_y = padded.shape[2] - 6
    extent_z = padded.shape[3] - 6
    shifted = []
    for k in range(len(speeds)):
        start_x = 3 - speeds[k][0]
        start_y = 3 - speeds[k][1]
        start_z = 3 - speeds[k][2]
        shifted.append(
            padded[
                k,
                start_x : start_x + extent_x,
                start_y : start_y + extent_y,
                start_z : start_z + extent_z,
            ]
        )
    return jnp.stack(shifted)


def body(populations, pore_mask):
    tables = lattice_tables()
    speeds = tables[5]
    state = populations
    collided = collide(state, pore_mask, tables)
    padded = extended(collided, (("gx", 1), ("gy", 2), ("gz", 3)), 3)
    state = stream(padded, speeds)
    return state


def solution(mesh):
    placed = (P(None, "gx", "gy", "gz"), P("gx", "gy", "gz"))
    return jax.shard_map(
        body, mesh=mesh, in_specs=placed, out_specs=P(None, "gx", "gy", "gz"), check_vma=False
    )
```

profile of v0, /device:TPU:0, one launch (start us, length us, event | category | flops | bytes accessed | tf_op | source)
XLA Modules:
  0.0 51.8 jit_solution(102857282368514262)
XLA Ops:
  0.0 0.9 %fusion.14 = (f32[1,3,4,128]{3,2,1,0:T(4,128)S(1)}, f32[1,3,4,128]{3,2,1,0:T(4,128)S(1)}, f32[1,3,4,128]{3,2,1,0:T(4,128)S(1)}, f32[1,3,4,128]{3,2,1,0:T(4,128)S...) fusion(f32[39,3,4,128]{3,2,1,0:T(4,128)} %param.7), kind=kLoop, calls=%fused_computation.66 | loop fusion | bytes 233472 | tf_op jit(solution)/shard_map/slice | solution.py:114
  0.9 0.9 %fusion.15 = (f32[1,3,4,128]{3,2,1,0:T(4,128)S(1)}, f32[1,3,4,128]{3,2,1,0:T(4,128)S(1)}, f32[1,3,4,128]{3,2,1,0:T(4,128)S(1)}, f32[1,3,4,128]{3,2,1,0:T(4,128)S...) fusion(f32[39,3,4,128]{3,2,1,0:T(4,128)} %param.7), kind=kLoop, calls=%fused_computation.67 | loop fusion | bytes 233472 | tf_op jit(solution)/shard_map/slice | solution.py:114
  1.8 1.0 %reshape.58 = f32[39,1536]{1,0:T(8,128)S(1)} reshape(f32[39,3,4,128]{3,2,1,0:T(4,128)} %param.7) | data formatting | bytes 479232 | tf_op jit(solution)/shard_map/reshape | solution.py:101
  2.9 0.7 %broadcast_compare_fusion = pred[3,4,128]{2,1,0:T(4,128)(4,1)S(1)} fusion(s32[3,4,128]{2,1,0:T(4,128)} %param.8), kind=kLoop, calls=%fused_computation.53 | loop fusion | flops 1536 | bytes 7680 | tf_op jit(solution)/shard_map/eq | solution.py:115
  3.6 1.0 %fusion.17 = f32[20,1536]{1,0:T(8,128)S(1)} fusion(f32[20,39]{1,0:T(8,128)} %constant.13.clone, f32[39,1536]{1,0:T(8,128)S(1)} %reshape.58), kind=kOutput, calls=%fused_computation.69 | convolution fusion | flops 14376960 | bytes 365616 | tf_op jit(solution)/shard_map/dot_general | solution.py:102
  6.2 3.1 %collective-permute-start.1 = (f32[39,3,4,128]{3,0,2,1:T(8,128)S(1)}, f32[39,3,4,128]{3,0,2,1:T(8,128)S(1)}, u32[]{:S(2)}, u32[]{:S(2)}) collective-permute-start(f32[39,3,4,128]{3,0,2,1:T(8,128)S(1)} %copy.8), channel_id=1, source_target_pairs={{0,4},{4,8},{8,12},{12,16},{16,20},{20,24},{24,28},{28,0},{1,5},{5... | collective-permute-start | bytes 718856 | tf_op jit(solution)/shard_map/ppermute | solution.py:30
  9.2 3.1 %collective-permute-start = (f32[39,3,4,128]{3,0,2,1:T(8,128)S(1)}, f32[39,3,4,128]{3,0,2,1:T(8,128)S(1)}, u32[]{:S(2)}, u32[]{:S(2)}) collective-permute-start(f32[39,3,4,128]{3,0,2,1:T(8,128)S(1)} %copy.8), channel_id=1, source_target_pairs={{4,0},{8,4},{12,8},{16,12},{20,16},{24,20},{28,24},{0,28},{5,1},{9... | collective-permute-start | bytes 718856 | tf_op jit(solution)/shard_map/ppermute | solution.py:32
  12.3 7.4 %collective-permute-done.1 = f32[39,3,4,128]{3,0,2,1:T(8,128)S(1)} collective-permute-done((f32[39,3,4,128]{3,0,2,1:T(8,128)S(1)}, f32[39,3,4,128]{3,0,2,1:T(8,128)S(1)}, u32[]{:S(2)}, u32[]{:S(2)}) %collective-permute-start.1) | collective-permute-done | bytes 239648 | tf_op jit(solution)/shard_map/ppermute | solution.py:30
  19.8 2.1 %collective-permute-done = f32[39,3,4,128]{3,0,2,1:T(8,128)S(1)} collective-permute-done((f32[39,3,4,128]{3,0,2,1:T(8,128)S(1)}, f32[39,3,4,128]{3,0,2,1:T(8,128)S(1)}, u32[]{:S(2)}, u32[]{:S(2)}) %collective-permute-start) | collective-permute-done | bytes 239648 | tf_op jit(solution)/shard_map/ppermute | solution.py:32
  23.2 0.6 %slice.554 = f32[1,3,4,128]{3,0,2,1:T(1,128)} slice(f32[39,3,4,128]{3,0,2,1:T(8,128)S(1)} %collective-permute-done.1), slice={[38:39], [0:3], [0:4], [0:128]} | slice | bytes 12288 | tf_op jit(solution)/shard_map/slice | solution.py:128
  24.4 0.6 %fusion.12 = (f32[1,3,4,128]{3,0,2,1:T(1,128)}, f32[1,3,4,128]{3,0,2,1:T(1,128)}) fusion(f32[39,6,4,128]{3,0,2,1:T(8,128)S(1)} %get-tuple-element.62), kind=kLoop, calls=%fused_computation.64 | loop fusion | bytes 24576 | tf_op jit(solution)/shard_map/slice | solution.py:128
  25.6 0.8 %copy-done = f32[39,9,3,128]{3,0,2,1:T(8,128)} copy-done((f32[39,9,3,128]{3,0,2,1:T(8,128)}, f32[39,9,3,128]{3,0,2,1:T(8,128)S(1)}, u32[]{:S(2)}) %copy-start) | copy-done | bytes 539160
  26.6 1.9 %fusion.10 = (f32[39,9,10,3]{3,0,2,1:T(8,128)}, f32[39,9,10,3]{3,0,2,1:T(8,128)S(1)}) fusion(f32[39,9,10,128]{3,0,2,1:T(8,128)S(1)} %pad_maximum_fusion), kind=kLoop, calls=%fused_computation.62 | loop fusion | bytes 168480 | tf_op jit(solution)/shard_map/slice | solution.py:27
  28.4 2.9 %copy.14 = f32[39,9,10,3]{0,3,2,1:T(4,128)} copy(f32[39,9,10,3]{3,0,2,1:T(8,128)} %get-tuple-element.40) | data formatting | bytes 84240 | tf_op jit(solution)/shard_map/slice | solution.py:27
  31.3 0.7 %copy.11 = f32[39,9,10,3]{0,3,2,1:T(4,128)S(1)} copy(f32[39,9,10,3]{3,0,2,1:T(8,128)S(1)} %get-tuple-element.41) | data formatting | bytes 84240 | tf_op jit(solution)/shard_map/slice | solution.py:26
  32.1 1.6 %collective-permute-start.4 = (f32[39,9,10,3]{0,3,2,1:T(4,128)S(1)}, f32[39,9,10,3]{0,3,2,1:T(4,128)S(1)}, u32[]{:S(2)}, u32[]{:S(2)}) collective-permute-start(f32[39,9,10,3]{0,3,2,1:T(4,128)S(1)} %copy.11), channel_id=1, source_target_pairs={{1,0},{0,1},{3,2},{2,3},{5,4},{4,5},{7,6},{6,7},{9,8},{8,9},{11,10... | collective-permute-start | bytes 126368 | tf_op jit(solution)/shard_map/ppermute | solution.py:32
  34.2 8.6 %collective-permute-done.5 = f32[39,9,10,3]{0,3,2,1:T(4,128)} collective-permute-done((f32[39,9,10,3]{0,3,2,1:T(4,128)}, f32[39,9,10,3]{0,3,2,1:T(4,128)}, u32[]{:S(2)}, u32[]{:S(2)}) %collective-permute-start.5) | collective-permute-done | bytes 42152 | tf_op jit(solution)/shard_map/ppermute | solution.py:30
  42.8 1.7 %copy.15 = f32[39,9,10,3]{3,0,2,1:T(8,128)S(1)} copy(f32[39,9,10,3]{0,3,2,1:T(4,128)} %collective-permute-done.5) | data formatting | bytes 84240 | tf_op jit(solution)/shard_map/ppermute | solution.py:30
  44.5 1.6 %pad_maximum_fusion.18 = (f32[1,3,4,128]{3,0,2,1:T(1,128)}, f32[1,3,4,128]{3,0,2,1:T(1,128)}, f32[1,3,4,128]{3,0,2,1:T(1,128)}, f32[1,3,4,128]{3,0,2,1:T(1,128)}, f32[1,3,4,128]{3,0,2,1:T(1,128)}) fusion(f32[39,9,10,3]{3,0,2,1:T(8,128)S(1)} %copy.15, f32[39,9,3,128]{3,0,2,1:T(8,128)} %copy-done, f32[39,9,4,128]{3,0,2,1:T(8,128)S(1)} %get-tuple-element.61, ...), kind=kLoop, calls=%fused_computation.31 | loop fusion | flops 19968 | bytes 1869960 | tf_op jit(solution)/shard_map/slice | solution.py:128
  46.1 0.8 %pad_maximum_fusion.2 = (f32[1,3,4,128]{3,0,2,1:T(1,128)}, f32[1,3,4,128]{3,0,2,1:T(1,128)}, f32[1,3,4,128]{3,0,2,1:T(1,128)}, f32[1,3,4,128]{3,0,2,1:T(1,128)}, f32[1,3,4,128]{3,0,2,1:T(1,128)}) fusion(f32[39,9,10,3]{3,0,2,1:T(8,128)S(1)} %copy.15, f32[39,9,3,128]{3,0,2,1:T(8,128)S(1)} %copy-done.1, f32[39,9,4,128]{3,0,2,1:T(8,128)S(1)} %get-tuple-element.61, ...), kind=kLoop, calls=%fused_computation.15 | loop fusion | flops 19968 | bytes 1869960 | tf_op jit(solution)/shard_map/concatenate | solution.py:28
  46.9 0.7 %pad_maximum_fusion.29 = (f32[1,3,4,128]{3,0,2,1:T(1,128)S(1)}, f32[1,3,4,128]{3,0,2,1:T(1,128)}, f32[1,3,4,128]{3,0,2,1:T(1,128)}, f32[1,3,4,128]{3,0,2,1:T(1,128)}) fusion(f32[39,9,10,3]{3,0,2,1:T(8,128)S(1)} %copy.15, f32[39,9,3,128]{3,0,2,1:T(8,128)S(1)} %copy-done.1, f32[39,9,4,128]{3,0,2,1:T(8,128)S(1)} %get-tuple-element.61, ...), kind=kLoop, calls=%fused_computation.42 | loop fusion | flops 15360 | bytes 1863816 | tf_op jit(solution)/shard_map/slice | solution.py:128
  47.6 0.8 %copy.12 = f32[39,9,10,3]{3,0,2,1:T(8,128)S(1)} copy(f32[39,9,10,3]{0,3,2,1:T(4,128)S(1)} %collective-permute-done.4) | data formatting | bytes 84240 | tf_op jit(solution)/shard_map/ppermute | solution.py:32
  48.4 0.9 %pad_maximum_fusion.30 = (f32[1,3,4,128]{3,0,2,1:T(1,128)S(1)}, f32[1,3,4,128]{3,0,2,1:T(1,128)S(1)}, f32[1,3,4,128]{3,0,2,1:T(1,128)S(1)}) fusion(f32[39,9,10,3]{3,0,2,1:T(8,128)S(1)} %copy.12, f32[39,9,3,128]{3,0,2,1:T(8,128)} %copy-done, f32[39,9,4,128]{3,0,2,1:T(8,128)S(1)} %get-tuple-element.61, f32[39,9,3,128]{3,0,2,1:T(8,128)S(1)} %collective-permute-done.3), kind=kLoop, calls=%fused_computation.43 | loop fusion | flops 13824 | bytes 1857672 | tf_op jit(solution)/shard_map/slice | solution.py:128
  51.0 0.8 %copy.18 = f32[39,3,4,128]{3,2,1,0:T(4,128)} copy(f32[39,3,4,128]{3,0,2,1:T(8,128)S(1)} %stack.8) | data formatting | bytes 479232 | tf_op jit(solution)/shard_map/stack | solution.py:135
  (84 shorter events, 6.3 us)
Async XLA Ops:
  0.0 4.9 %copy-start.25 = (f32[20]{0:T(128)S(1)}, f32[20]{0:T(128)}, u32[]{:S(2)}) copy-start(f32[20]{0:T(128)} %constant.16.clone) | copy-start | bytes 244
  0.0 4.9 %copy-start.26 = (f32[20]{0:T(128)S(1)}, f32[20]{0:T(128)}, u32[]{:S(2)}) copy-start(f32[20]{0:T(128)} %constant.15.clone) | copy-start | bytes 244
  0.0 4.9 %copy-start.24 = (f32[20,20]{1,0:T(8,128)S(1)}, f32[20,20]{1,0:T(8,128)}, u32[]{:S(2)}) copy-start(f32[20,20]{1,0:T(8,128)} %constant.14.clone) | copy-start | bytes 4804
  0.0 5.7 %copy-start.23 = (f32[39,20]{1,0:T(8,128)S(1)}, f32[39,20]{1,0:T(8,128)}, u32[]{:S(2)}) copy-start(f32[39,20]{1,0:T(8,128)} %constant.12.clone) | copy-start | bytes 9364
  0.0 5.3 %slice-start = ((f32[39,3,4,128]{3,2,1,0:T(4,128)}), f32[1,3,4,128]{3,2,1,0:T(4,128)S(1)}, s32[]{:S(2)}) async-start(f32[39,3,4,128]{3,2,1,0:T(4,128)} %param.7), calls=%async_computation | async-start | bytes 12288 | tf_op jit(solution)/shard_map/slice | solution.py:114
  6.2 13.5 %collective-permute-start.1 = (f32[39,3,4,128]{3,0,2,1:T(8,128)S(1)}, f32[39,3,4,128]{3,0,2,1:T(8,128)S(1)}, u32[]{:S(2)}, u32[]{:S(2)}) collective-permute-start(f32[39,3,4,128]{3,0,2,1:T(8,128)S(1)} %copy.8), channel_id=1, source_target_pairs={{0,4},{4,8},{8,12},{12,16},{16,20},{20,24},{24,28},{28,0},{1,5},{5... | collective-permute-start | bytes 718856 | tf_op jit(solution)/shard_map/ppermute | solution.py:30
  9.2 12.7 %collective-permute-start = (f32[39,3,4,128]{3,0,2,1:T(8,128)S(1)}, f32[39,3,4,128]{3,0,2,1:T(8,128)S(1)}, u32[]{:S(2)}, u32[]{:S(2)}) collective-permute-start(f32[39,3,4,128]{3,0,2,1:T(8,128)S(1)} %copy.8), channel_id=1, source_target_pairs={{4,0},{8,4},{12,8},{16,12},{20,16},{24,20},{28,24},{0,28},{5,1},{9... | collective-permute-start | bytes 718856 | tf_op jit(solution)/shard_map/ppermute | solution.py:32
  22.0 3.6 %collective-permute-start.3 = (f32[39,9,3,128]{3,0,2,1:T(8,128)S(1)}, f32[39,9,3,128]{3,0,2,1:T(8,128)S(1)}, u32[]{:S(2)}, u32[]{:S(2)}) collective-permute-start(f32[39,9,3,128]{3,0,2,1:T(8,128)S(1)} %get-tuple-element.52), channel_id=1, source_target_pairs={{0,2},{2,0},{1,3},{3,1},{4,6},{6,4},{5,7},{7,5},{8,10},{10,8},{9,1... | collective-permute-start | bytes 1617416 | tf_op jit(solution)/shard_map/ppermute | solution.py:30
  22.1 3.5 %collective-permute-start.2 = (f32[39,9,3,128]{3,0,2,1:T(8,128)S(1)}, f32[39,9,3,128]{3,0,2,1:T(8,128)S(1)}, u32[]{:S(2)}, u32[]{:S(2)}) collective-permute-start(f32[39,9,3,128]{3,0,2,1:T(8,128)S(1)} %get-tuple-element.53), channel_id=1, source_target_pairs={{2,0},{0,2},{3,1},{1,3},{6,4},{4,6},{7,5},{5,7},{10,8},{8,10},{11,... | collective-permute-start | bytes 1617416 | tf_op jit(solution)/shard_map/ppermute | solution.py:32
  25.6 0.8 %copy-start = (f32[39,9,3,128]{3,0,2,1:T(8,128)}, f32[39,9,3,128]{3,0,2,1:T(8,128)S(1)}, u32[]{:S(2)}) copy-start(f32[39,9,3,128]{3,0,2,1:T(8,128)S(1)} %collective-permute-done.2) | copy-start | bytes 1617412
  32.1 15.5 %collective-permute-start.4 = (f32[39,9,10,3]{0,3,2,1:T(4,128)S(1)}, f32[39,9,10,3]{0,3,2,1:T(4,128)S(1)}, u32[]{:S(2)}, u32[]{:S(2)}) collective-permute-start(f32[39,9,10,3]{0,3,2,1:T(4,128)S(1)} %copy.11), channel_id=1, source_target_pairs={{1,0},{0,1},{3,2},{2,3},{5,4},{4,5},{7,6},{6,7},{9,8},{8,9},{11,10... | collective-permute-start | bytes 126368 | tf_op jit(solution)/shard_map/ppermute | solution.py:32
  33.6 9.2 %collective-permute-start.5 = (f32[39,9,10,3]{0,3,2,1:T(4,128)}, f32[39,9,10,3]{0,3,2,1:T(4,128)}, u32[]{:S(2)}, u32[]{:S(2)}) collective-permute-start(f32[39,9,10,3]{0,3,2,1:T(4,128)} %copy.14), channel_id=1, source_target_pairs={{0,1},{1,0},{2,3},{3,2},{4,5},{5,4},{6,7},{7,6},{8,9},{9,8},{10,11... | collective-permute-start | bytes 126368 | tf_op jit(solution)/shard_map/ppermute | solution.py:30
  44.5 1.6 %copy-start.1 = (f32[39,9,3,128]{3,0,2,1:T(8,128)S(1)}, f32[39,9,3,128]{3,0,2,1:T(8,128)}, u32[]{:S(2)}) copy-start(f32[39,9,3,128]{3,0,2,1:T(8,128)} %copy-done) | copy-start | bytes 1617412
  48.3 1.1 %copy-start.2 = (f32[39,9,3,128]{3,0,2,1:T(8,128)S(1)}, f32[39,9,3,128]{3,0,2,1:T(8,128)}, u32[]{:S(2)}) copy-start(f32[39,9,3,128]{3,0,2,1:T(8,128)} %copy-done) | copy-start | bytes 1617412
  49.7 0.8 %copy-start.13 = (f32[1,3,4,128]{3,0,2,1:T(1,128)S(1)}, f32[1,3,4,128]{3,0,2,1:T(1,128)}, u32[]{:S(2)}) copy-start(f32[1,3,4,128]{3,0,2,1:T(1,128)} %get-tuple-element.26) | copy-start | bytes 18436
  49.7 0.8 %copy-start.14 = (f32[1,3,4,128]{3,0,2,1:T(1,128)S(1)}, f32[1,3,4,128]{3,0,2,1:T(1,128)}, u32[]{:S(2)}) copy-start(f32[1,3,4,128]{3,0,2,1:T(1,128)} %get-tuple-element.27) | copy-start | bytes 18436
  49.7 0.8 %copy-start.15 = (f32[1,3,4,128]{3,0,2,1:T(1,128)S(1)}, f32[1,3,4,128]{3,0,2,1:T(1,128)}, u32[]{:S(2)}) copy-start(f32[1,3,4,128]{3,0,2,1:T(1,128)} %get-tuple-element.28) | copy-start | bytes 18436
  49.7 0.8 %copy-start.16 = (f32[1,3,4,128]{3,0,2,1:T(1,128)S(1)}, f32[1,3,4,128]{3,0,2,1:T(1,128)}, u32[]{:S(2)}) copy-start(f32[1,3,4,128]{3,0,2,1:T(1,128)} %get-tuple-element.29) | copy-start | bytes 18436
  49.7 0.8 %copy-start.17 = (f32[1,3,4,128]{3,0,2,1:T(1,128)S(1)}, f32[1,3,4,128]{3,0,2,1:T(1,128)}, u32[]{:S(2)}) copy-start(f32[1,3,4,128]{3,0,2,1:T(1,128)} %get-tuple-element.49) | copy-start | bytes 18436
  49.7 0.8 %copy-start.18 = (f32[1,3,4,128]{3,0,2,1:T(1,128)S(1)}, f32[1,3,4,128]{3,0,2,1:T(1,128)}, u32[]{:S(2)}) copy-start(f32[1,3,4,128]{3,0,2,1:T(1,128)} %get-tuple-element.18) | copy-start | bytes 18436
  49.8 0.8 %copy-start.19 = (f32[1,3,4,128]{3,0,2,1:T(1,128)S(1)}, f32[1,3,4,128]{3,0,2,1:T(1,128)}, u32[]{:S(2)}) copy-start(f32[1,3,4,128]{3,0,2,1:T(1,128)} %get-tuple-element.19) | copy-start | bytes 18436
  49.8 0.8 %copy-start.20 = (f32[1,3,4,128]{3,0,2,1:T(1,128)S(1)}, f32[1,3,4,128]{3,0,2,1:T(1,128)}, u32[]{:S(2)}) copy-start(f32[1,3,4,128]{3,0,2,1:T(1,128)} %get-tuple-element.20) | copy-start | bytes 18436
  49.8 0.8 %copy-start.21 = (f32[1,3,4,128]{3,0,2,1:T(1,128)S(1)}, f32[1,3,4,128]{3,0,2,1:T(1,128)}, u32[]{:S(2)}) copy-start(f32[1,3,4,128]{3,0,2,1:T(1,128)} %get-tuple-element.21) | copy-start | bytes 18436
  49.8 0.8 %copy-start.22 = (f32[1,3,4,128]{3,0,2,1:T(1,128)S(1)}, f32[1,3,4,128]{3,0,2,1:T(1,128)}, u32[]{:S(2)}) copy-start(f32[1,3,4,128]{3,0,2,1:T(1,128)} %get-tuple-element.47) | copy-start | bytes 18436
  (10 other events, 7.2 us)
where the time goes:
time: 52.2 us; the launch traced here: 51.8 us
  waiting for transfers between devices  18.1 us (35%)
  local copies, waits for them, and re-layouts  17.5 us (34%)
  starting transfers between devices  8.82 us (17%)
  other arithmetic  5.32 us (10%)
  matrix products  1.64 us (3%)
    ppermute x3, waiting for transfers between devices, extended(): lax.ppermute(tail, axis, [(i, (i + 1) % count) for i in range(count)])  16 us
    ppermute x3, starting transfers between devices, extended(): lax.ppermute(head, axis, [((i + 1) % count, i) for i in range(count)])  5.15 us
    slice x3, local copies, waits for them, and re-layouts, extended(): lax.slice_in_dim(cells, cells.shape[dim] - width, cells.shape[dim], axis=...  4.84 us
    ppermute x3, starting transfers between devices, extended(): lax.ppermute(tail, axis, [(i, (i + 1) % count) for i in range(count)])  3.67 us
    slice x4, other arithmetic, stream(): padded[k, start_x:start_x + extent_x, start_y:start_y + extent_y, start_z...  3.42 us
    slice x5, local copies, waits for them, and re-layouts, stream(): padded[k, start_x:start_x + extent_x, start_y:start_y + extent_y, start_z...  3 us
    ppermute x3, waiting for transfers between devices, extended(): lax.ppermute(head, axis, [((i + 1) % count, i) for i in range(count)])  2.11 us
    slice x4, local copies, waits for them, and re-layouts, collide(): mirrored = jnp.stack([columns[opposite[k]] for k in range(pop_count)])  1.79 us
  transfers between devices with their start and end apart: 6, of which 3 were waited for; matrix products, arithmetic and copies ran while one was open for 15% of the time, Pallas kernels for 0%

commit v1 on v0

v1 whole, which is shorter than its diff:
```python
import functools

import jax
import jax.numpy as jnp
from jax import lax
from jax.experimental import pallas as pl
from jax.experimental.pallas import tpu as pltpu
from jax.sharding import PartitionSpec as P

MESH = pl.DeviceIdType.MESH

sound_sq = 2.0 / 3.0
relax_time = 0.8
pair_list = [(0, 0), (1, 1), (2, 2), (0, 1), (0, 2), (1, 2)]
triple_list = [
    (0, 0, 0),
    (1, 1, 1),
    (2, 2, 2),
    (0, 0, 1),
    (0, 0, 2),
    (1, 1, 0),
    (1, 1, 2),
    (2, 2, 0),
    (2, 2, 1),
    (0, 1, 2),
]
shell_weights = {
    (0, 0, 0): 1.0 / 12.0,
    (0, 0, 1): 1.0 / 12.0,
    (1, 1, 1): 1.0 / 27.0,
    (0, 0, 2): 2.0 / 135.0,
    (0, 2, 2): 1.0 / 432.0,
    (0, 0, 3): 1.0 / 1620.0,
}


def lattice():
    speeds = []
    weights = []
    for a in range(-3, 4):
        for b in range(-3, 4):
            for c in range(-3, 4):
                pattern = tuple(sorted((abs(a), abs(b), abs(c))))
                if pattern in shell_weights:
                    speeds.append((a, b, c))
                    weights.append(shell_weights[pattern])
    return speeds, weights


speeds, weights = lattice()
opposite = [speeds.index((-v[0], -v[1], -v[2])) for v in speeds]


def accumulate(total, factor, term):
    if factor == 0:
        return total
    if total is None:
        return term if factor == 1 else factor * term
    if factor == 1:
        return total + term
    if factor == -1:
        return total - term
    return total + factor * term


def collide(load, pore):
    rest = speeds.index((0, 0, 0))
    pairs = [(k, opposite[k]) for k in range(len(speeds)) if k > opposite[k]]
    density = weights[rest] * load(rest)
    first = [None] * 3
    second = {ab: None for ab in pair_list}
    third = {abc: None for abc in triple_list}
    for shell in shell_weights:
        members = [(k, o) for k, o in pairs if tuple(sorted(map(abs, speeds[k]))) == shell]
        if not members:
            continue
        part0, part1 = None, [None] * 3
        part2 = {ab: None for ab in pair_list}
        part3 = {abc: None for abc in triple_list}
        for k, o in members:
            v = speeds[k]
            even = load(k) + load(o)
            odd = load(k) - load(o)
            part0 = accumulate(part0, 1, even)
            for a, b in pair_list:
                part2[a, b] = accumulate(part2[a, b], v[a] * v[b], even)
            for a in range(3):
                part1[a] = accumulate(part1[a], v[a], odd)
            for a, b, c in triple_list:
                part3[a, b, c] = accumulate(part3[a, b, c], v[a] * v[b] * v[c], odd)
        w = shell_weights[shell]
        density = accumulate(density, w, part0)
        for a in range(3):
            first[a] = accumulate(first[a], w, part1[a])
        for ab in pair_list:
            if part2[ab] is not None:
                second[ab] = accumulate(second[ab], w, part2[ab])
        for abc in triple_list:
            if part3[abc] is not None:
                third[abc] = accumulate(third[abc], w, part3[abc])

    u = [first[a] / density for a in range(3)]
    relax = 1.0 - 1.0 / relax_time
    const = density
    linear = [first[a] * (1.0 / sound_sq) for a in range(3)]
    quad, cubic = {}, {}
    flux = {}
    for a, b in pair_list:
        flux[a, b] = first[a] * u[b]
        moment = second[a, b]
        if a == b:
            moment = moment - sound_sq * density
        scale = (1.0 if a == b else 2.0) / (2.0 * sound_sq**2)
        quad[a, b] = (scale * (1.0 - relax)) * flux[a, b] + (scale * relax) * moment
        if a == b:
            const = const - sound_sq * quad[a, b]
    for a, b, c in triple_list:
        moment = third[a, b, c]
        if a == b == c:
            moment = moment - (3.0 * sound_sq) * first[a]
        elif a == b:
            moment = moment - sound_sq * first[c]
        pair = (a, b) if (a, b) in flux else (b, a)
        scale = {1: 1.0, 2: 3.0, 3: 6.0}[len({a, b, c})] / (6.0 * sound_sq**3)
        cubic[a, b, c] = (scale * (1.0 - relax)) * (flux[pair] * u[c]) + (scale * relax) * moment
        if a == b == c:
            linear[a] = linear[a] - (3.0 * sound_sq) * cubic[a, b, c]
        elif a == b:
            linear[c] = linear[c] - sound_sq * cubic[a, b, c]

    yield rest, jnp.where(pore, const, load(rest))
    for k, o in pairs:
        v = speeds[k]
        even, odd = const, None
        for a, b in pair_list:
            even = accumulate(even, float(v[a] * v[b]), quad[a, b])
        for a in range(3):
            odd = accumulate(odd, float(v[a]), linear[a])
        for a, b, c in triple_list:
            odd = accumulate(odd, float(v[a] * v[b] * v[c]), cubic[a, b, c])
        yield k, jnp.where(pore, even + odd, load(o))
        yield o, jnp.where(pore, even - odd, load(k))


def cut(speed, extent):
    if speed >= 0:
        return (0, extent - speed), (speed, extent), (extent - speed, extent), (0, speed)
    return (-speed, extent), (0, extent + speed), (0, -speed), (extent + speed, extent)


def merge_key(speed, extent):
    return abs(speed) if 2 * abs(speed) <= extent else speed


def make_plan(nx, ny):
    sizes, slots, pieces = {}, {}, []
    for k, (cx, cy, cz) in enumerate(speeds):
        stay_from, stay_to, leave_from, leave_to = cut(cx, nx)
        own = []
        for source, land, dx in ((stay_from, stay_to, 0), (leave_from, leave_to, (cx > 0) - (cx < 0))):
            count = source[1] - source[0]
            if count == 0:
                continue
            where = {}
            for oy in (0, 1):
                for oz in (0, 1):
                    if (oy and not cy) or (oz and not cz) or (dx, oy, oz) == (0, 0, 0):
                        continue
                    key = (
                        dx,
                        oy,
                        oz,
                        cx,
                        merge_key(cy, ny) if oy else (cy,),
                        abs(cz) if oz else (cz,),
                    )
                    if key not in slots:
                        slots[key] = sizes.get((dx, oy, oz), 0)
                        sizes[dx, oy, oz] = slots[key] + count
                    where[oy, oz] = slots[key]
            own.append((source, land, dx, where))
        pieces.append(own)
    return sizes, pieces


def neighbours(count):
    return (1,) if count == 2 else (1, -1)


def step_kernel(counts, sizes, pieces, messages, names, pop_ref, mask_ref, out_ref, *scratch):
    nx, ny, nz = out_ref.shape[1:]
    send = dict(zip(names, scratch[: len(names)]))
    recv = dict(zip(messages, scratch[len(names) : len(names) + len(messages)]))
    send_sem, recv_sem = scratch[len(names) + len(messages) :]
    here = [lax.axis_index(axis) for axis in ("gx", "gy", "gz")]

    def target(step):
        return {
            axis: lax.rem(at + (s + count), count)
            for axis, at, s, count in zip(("gx", "gy", "gz"), here, step, counts)
            if s
        }

    barrier = pltpu.get_barrier_semaphore()
    for step in messages:
        pl.semaphore_signal(barrier, inc=1, device_id=target(step), device_id_type=MESH)

    def block(span, rows, lanes):
        return (slice(*span), slice(*rows), slice(*lanes))

    pore = mask_ref[...] == 1
    every_lane = (0, nz)
    for k, plane in collide(lambda j: pop_ref[j], pore):
        cx, cy, cz = speeds[k]
        if cz:
            plane = pltpu.roll(plane, cz % nz, 2)
        y_stay, y_land, y_leave, y_wrap = cut(cy, ny)
        z_wrap = cut(cz, nz)[3]
        for source, land, dx, where in pieces[k]:
            count = source[1] - source[0]
            value = plane[slice(*source)]
            kept = value[:, slice(*y_stay)]
            if dx == 0:
                out_ref[(k,) + block(land, y_land, every_lane)] = kept
            else:
                at = where[0, 0]
                send[dx, 0, 0][block((at, at + count), y_land, every_lane)] = kept
            if cy:
                at = where[1, 0]
                moved = value[:, slice(*y_leave)]
                send[dx, 1, 0][block((at, at + count), y_wrap, every_lane)] = moved
            if cz:
                at = where[0, 1]
                send[dx, 0, 1][block((at, at + count), y_land, z_wrap)] = kept[:, :, slice(*z_wrap)]
            if cy and cz:
                at = where[1, 1]
                send[dx, 1, 1][block((at, at + count), y_wrap, z_wrap)] = moved[:, :, slice(*z_wrap)]

    pl.semaphore_wait(barrier, len(messages))
    copies = {}
    for number, step in enumerate(messages):
        kind = (step[0], abs(step[1]), abs(step[2]))
        copies[step] = pltpu.make_async_remote_copy(
            src_ref=send[kind],
            dst_ref=recv[step],
            send_sem=send_sem.at[number],
            recv_sem=recv_sem.at[number],
            device_id=target(step),
            device_id_type=MESH,
        )
        copies[step].start()

    def came_by(step, speed):
        return step == 0 or step * speed > 0

    for step in reversed(messages):
        copies[step].wait_recv()
        got = recv[step]
        dx, sy, sz = step
        for k, (cx, cy, cz) in enumerate(speeds):
            if (sy and not cy) or (sz and not cz):
                continue
            if counts[1] != 2 and not came_by(sy, cy):
                continue
            if counts[2] != 2 and not came_by(sz, cz):
                continue
            _, y_land, _, y_wrap = cut(cy, ny)
            rows = y_wrap if sy else y_land
            lanes = cut(cz, nz)[3] if sz else every_lane
            for source, land, piece_dx, where in pieces[k]:
                if piece_dx != dx:
                    continue
                at = where[abs(sy), abs(sz)]
                span = (at, at + source[1] - source[0])
                out_ref[(k,) + block(land, rows, lanes)] = got[block(span, rows, lanes)]
    for step in messages:
        copies[step].wait_send()


def body(counts, populations, pore_mask):
    nx, ny, nz = populations.shape[1:]
    sizes, pieces = make_plan(nx, ny)
    names = sorted(sizes)
    messages = []
    for dx, oy, oz in [(dx, oy, oz) for oz in (1, 0) for oy in (1, 0) for dx in (1, -1)] + [
        (0, 1, 1),
        (0, 0, 1),
        (0, 1, 0),
    ]:
        for sy in neighbours(counts[1]) if oy else (0,):
            for sz in neighbours(counts[2]) if oz else (0,):
                messages.append((dx, sy, sz))
    kernel = functools.partial(step_kernel, counts, sizes, pieces, messages, names)
    shape = lambda name: pltpu.VMEM((sizes[name[0], abs(name[1]), abs(name[2])], ny, nz), jnp.float32)
    return pl.pallas_call(
        kernel,
        out_shape=jax.ShapeDtypeStruct(populations.shape, populations.dtype),
        in_specs=[pl.BlockSpec(memory_space=pltpu.VMEM)] * 2,
        out_specs=pl.BlockSpec(memory_space=pltpu.VMEM),
        scratch_shapes=[shape(name) for name in names]
        + [shape(step) for step in messages]
        + [pltpu.SemaphoreType.DMA((len(messages),)), pltpu.SemaphoreType.DMA((len(messages),))],
        compiler_params=pltpu.CompilerParams(collective_id=0, has_side_effects=True),
    )(populations, pore_mask)


def solution(mesh):
    counts = tuple(mesh.shape[axis] for axis in ("gx", "gy", "gz"))
    placed = (P(None, "gx", "gy", "gz"), P("gx", "gy", "gz"))
    return jax.shard_map(
        functools.partial(body, counts),
        mesh=mesh,
        in_specs=placed,
        out_specs=P(None, "gx", "gy", "gz"),
        check_vma=False,
    )
```

time: 52.2 us -> 13.8 us (0.26)
  waiting for transfers between devices: 18.1 us -> 0 us
  local copies, waits for them, and re-layouts: 17.5 us -> 1.66 us
  Pallas kernels: 0 us -> 12 us
  starting transfers between devices: 8.82 us -> 0 us
  other arithmetic: 5.32 us -> 0 us
  matrix products: 1.64 us -> 0 us
    ppermute x6 -> x0, waiting for transfers between devices: 18.1 us -> none  [the longest x3 16 us: extended(): lax.ppermute(tail, axis, [(i, (i + 1) % count) for i in range(count)])]
    pallas_call x0 -> x1, Pallas kernels: none -> 12 us  [body(): pl.pallas_call(kernel, out_shape=jax.ShapeDtypeStruct(populations.shape,...]
    slice x13 -> x0, local copies, waits for them, and re-layouts: 10.4 us -> none  [the longest x3 4.84 us: extended(): lax.slice_in_dim(cells, cells.shape[dim] - width, cells.shape[dim], axis=...]
    ppermute x6 -> x0, starting transfers between devices: 8.82 us -> none  [the longest x3 5.15 us: extended(): lax.ppermute(head, axis, [((i + 1) % count, i) for i in range(count)])]
    slice x4 -> x0, other arithmetic: 3.42 us -> none  [stream(): padded[k, start_x:start_x + extent_x, start_y:start_y + extent_y, start_z...]
    ppermute x2 -> x0, local copies, waits for them, and re-layouts: 2.43 us -> none  [the longest x1 1.67 us: extended(): lax.ppermute(tail, axis, [(i, (i + 1) % count) for i in range(count)])]
    another operation x4 -> x0, local copies, waits for them, and re-layouts: 1.78 us -> none  [the longest x2 1.16 us: stream(): return jnp.stack(shifted)]
    dot_general x3 -> x0, matrix products: 1.64 us -> none  [the longest x1 0.96 us: collide(): moments = jnp.dot(project, columns, precision=lax.Precision.HIGHEST)]
  transfers between devices with their start and end apart: 6 -> 0, of which waited for: 3 -> 0; matrix products, arithmetic and copies ran while one was open for 15% -> 0% of each run, Pallas kernels for 0% -> 0%
where the time goes in v1:
time: 13.8 us; the launch traced here: 13.7 us
  Pallas kernels  12 us (87%)
  local copies, waits for them, and re-layouts  1.66 us (12%)
    pallas_call x1, Pallas kernels, body(): pl.pallas_call(kernel, out_shape=jax.ShapeDtypeStruct(populations.shape,...  12 us
    unnamed x1, local copies, waits for them, and re-layouts  1.66 us

profile of v1, /device:TPU:0, one launch (start us, length us, event | category | flops | bytes accessed | tf_op | source)
XLA Modules:
  0.0 13.7 jit_solution(5880968480006143071)
XLA Ops:
  0.0 12.0 %shard_map.28 = f32[39,3,4,128]{3,2,1,0:T(4,128)} custom-call(f32[39,3,4,128]{3,2,1,0:T(4,128)} %pop_ref.1, s32[3,4,128]{2,1,0:T(4,128)} %mask_ref.1), custom_call_target="tpu_custom_call" | custom-call | tf_op jit(solution)/shard_map/pallas_call | solution.py:295
  12.0 1.7 %copy.4 = f32[39,3,4,128]{3,2,1,0:T(4,128)} copy(f32[39,3,4,128]{3,2,1,0:T(4,128)} %shard_map.28) | data formatting | bytes 479232

commit v2 on v1

--- a/solution.py
+++ b/solution.py
@@ -187,8 +187,9 @@
     return (1,) if count == 2 else (1, -1)
 
 
-def step_kernel(counts, sizes, pieces, messages, names, pop_ref, mask_ref, out_ref, *scratch):
+def step_kernel(counts, sizes, pieces, messages, names, pop_hbm, mask_hbm, out_ref, *scratch):
     nx, ny, nz = out_ref.shape[1:]
+    *scratch, pop_ref, mask_ref, load_sem = scratch
     send = dict(zip(names, scratch[: len(names)]))
     recv = dict(zip(messages, scratch[len(names) : len(names) + len(messages)]))
     send_sem, recv_sem = scratch[len(names) + len(messages) :]
@@ -204,6 +205,15 @@
     barrier = pltpu.get_barrier_semaphore()
     for step in messages:
         pl.semaphore_signal(barrier, inc=1, device_id=target(step), device_id_type=MESH)
+
+    loads = [
+        pltpu.make_async_copy(pop_hbm, pop_ref, load_sem.at[0]),
+        pltpu.make_async_copy(mask_hbm, mask_ref, load_sem.at[1]),
+    ]
+    for load in loads:
+        load.start()
+    for load in loads:
+        load.wait()
 
     def block(span, rows, lanes):
         return (slice(*span), slice(*rows), slice(*lanes))
@@ -294,12 +304,17 @@
     shape = lambda name: pltpu.VMEM((sizes[name[0], abs(name[1]), abs(name[2])], ny, nz), jnp.float32)
     return pl.pallas_call(
         kernel,
-        out_shape=jax.ShapeDtypeStruct(populations.shape, populations.dtype),
-        in_specs=[pl.BlockSpec(memory_space=pltpu.VMEM)] * 2,
+        out_shape=pltpu.VMEM(populations.shape, populations.dtype),
+        in_specs=[pl.BlockSpec(memory_space=pl.ANY)] * 2,
         out_specs=pl.BlockSpec(memory_space=pltpu.VMEM),
         scratch_shapes=[shape(name) for name in names]
         + [shape(step) for step in messages]
-        + [pltpu.SemaphoreType.DMA((len(messages),)), pltpu.SemaphoreType.DMA((len(messages),))],
+        + [pltpu.SemaphoreType.DMA((len(messages),)), pltpu.SemaphoreType.DMA((len(messages),))]
+        + [
+            pltpu.VMEM(populations.shape, populations.dtype),
+            pltpu.VMEM(pore_mask.shape, pore_mask.dtype),
+            pltpu.SemaphoreType.DMA((2,)),
+        ],
         compiler_params=pltpu.CompilerParams(collective_id=0, has_side_effects=True),
     )(populations, pore_mask)
 

time: 13.8 us -> 11.2 us (0.81)
  Pallas kernels: 12 us -> 10.4 us
  local copies, waits for them, and re-layouts: 1.66 us -> 0.69 us
    pallas_call x1, Pallas kernels: 12 us -> 10.4 us  [body(): pl.pallas_call(kernel, out_shape=pltpu.VMEM(populations.shape, population...]
    unnamed x1, local copies, waits for them, and re-layouts: 1.66 us -> 0.69 us
where the time goes in v2:
time: 11.2 us; the launch traced here: 11.1 us
  Pallas kernels  10.4 us (93%)
  local copies, waits for them, and re-layouts  0.69 us (6%)
    pallas_call x1, Pallas kernels, body(): pl.pallas_call(kernel, out_shape=pltpu.VMEM(populations.shape, population...  10.4 us
    unnamed x1, local copies, waits for them, and re-layouts  0.69 us

profile of v2, /device:TPU:0, one launch (start us, length us, event | category | flops | bytes accessed | tf_op | source)
XLA Modules:
  0.0 11.1 jit_solution(5851573558631468303)
XLA Ops:
  0.0 10.4 %shard_map.28 = f32[39,3,4,128]{3,2,1,0:T(4,128)S(1)} custom-call(f32[39,3,4,128]{3,2,1,0:T(4,128)} %pop_hbm.1, s32[3,4,128]{2,1,0:T(4,128)} %mask_hbm.1), custom_call_target="tpu_custom_call" | custom-call | tf_op jit(solution)/shard_map/pallas_call | solution.py:305
  10.4 0.7 %copy.4 = f32[39,3,4,128]{3,2,1,0:T(4,128)} copy(f32[39,3,4,128]{3,2,1,0:T(4,128)S(1)} %shard_map.28) | data formatting | bytes 479232

commit v3 on v2

--- a/solution.py
+++ b/solution.py
@@ -128,8 +128,7 @@
         elif a == b:
             linear[c] = linear[c] - sound_sq * cubic[a, b, c]
 
-    yield rest, jnp.where(pore, const, load(rest))
-    for k, o in pairs:
+    for k, o in sorted(pairs, key=lambda pair: speeds[pair[0]][0] == 0):
         v = speeds[k]
         even, odd = const, None
         for a, b in pair_list:
@@ -140,6 +139,7 @@
             odd = accumulate(odd, float(v[a] * v[b] * v[c]), cubic[a, b, c])
         yield k, jnp.where(pore, even + odd, load(o))
         yield o, jnp.where(pore, even - odd, load(k))
+    yield rest, jnp.where(pore, const, load(rest))
 
 
 def cut(speed, extent):
@@ -192,7 +192,7 @@
     *scratch, pop_ref, mask_ref, load_sem = scratch
     send = dict(zip(names, scratch[: len(names)]))
     recv = dict(zip(messages, scratch[len(names) : len(names) + len(messages)]))
-    send_sem, recv_sem = scratch[len(names) + len(messages) :]
+    send_sem, recv_sem, ready = scratch[len(names) + len(messages) :]
     here = [lax.axis_index(axis) for axis in ("gx", "gy", "gz")]
 
     def target(step):
@@ -204,7 +204,8 @@
 
     barrier = pltpu.get_barrier_semaphore()
     for step in messages:
-        pl.semaphore_signal(barrier, inc=1, device_id=target(step), device_id_type=MESH)
+        if step[0] <= 0:
+            pl.semaphore_signal(barrier, inc=1, device_id=target(step), device_id_type=MESH)
 
     loads = [
         pltpu.make_async_copy(pop_hbm, pop_ref, load_sem.at[0]),
@@ -218,9 +219,29 @@
     def block(span, rows, lanes):
         return (slice(*span), slice(*rows), slice(*lanes))
 
+    copies = {}
+    for number, step in enumerate(messages):
+        kind = (step[0], abs(step[1]), abs(step[2]))
+        copies[step] = pltpu.make_async_remote_copy(
+            src_ref=send[kind],
+            dst_ref=recv[step],
+            send_sem=send_sem.at[number],
+            recv_sem=recv_sem.at[number],
+            device_id=target(step),
+            device_id_type=MESH,
+        )
+    above = sum(step[0] > 0 for step in messages)
+
     pore = mask_ref[...] == 1
     every_lane = (0, nz)
-    for k, plane in collide(lambda j: pop_ref[j], pore):
+    moving = sum(speed[0] != 0 for speed in speeds)
+    for done, (k, plane) in enumerate(collide(lambda j: pop_ref[j], pore)):
+        if done == moving:
+            pl.semaphore_wait(barrier, len(messages) - above)
+            for step in messages:
+                if step[0] > 0:
+                    pl.semaphore_signal(ready, inc=1, device_id=target(step), device_id_type=MESH)
+                    copies[step].start()
         cx, cy, cz = speeds[k]
         if cz:
             plane = pltpu.roll(plane, cz % nz, 2)
@@ -246,19 +267,13 @@
                 at = where[1, 1]
                 send[dx, 1, 1][block((at, at + count), y_wrap, z_wrap)] = moved[:, :, slice(*z_wrap)]
 
-    pl.semaphore_wait(barrier, len(messages))
-    copies = {}
-    for number, step in enumerate(messages):
-        kind = (step[0], abs(step[1]), abs(step[2]))
-        copies[step] = pltpu.make_async_remote_copy(
-            src_ref=send[kind],
-            dst_ref=recv[step],
-            send_sem=send_sem.at[number],
-            recv_sem=recv_sem.at[number],
-            device_id=target(step),
-            device_id_type=MESH,
-        )
-        copies[step].start()
+    for step in messages:
+        if step[0] == 0:
+            copies[step].start()
+    pl.semaphore_wait(ready, above)
+    for step in messages:
+        if step[0] < 0:
+            copies[step].start()
 
     def came_by(step, speed):
         return step == 0 or step * speed > 0
@@ -310,6 +325,7 @@
         scratch_shapes=[shape(name) for name in names]
         + [shape(step) for step in messages]
         + [pltpu.SemaphoreType.DMA((len(messages),)), pltpu.SemaphoreType.DMA((len(messages),))]
+        + [pltpu.SemaphoreType.REGULAR]
         + [
             pltpu.VMEM(populations.shape, populations.dtype),
             pltpu.VMEM(pore_mask.shape, pore_mask.dtype),

time: 11.2 us -> 11.1 us (level)
    pallas_call x1, Pallas kernels: 10.4 us -> 10.3 us  [body(): pl.pallas_call(kernel, out_shape=pltpu.VMEM(populations.shape, population...]
where the time goes in v3:
time: 11.1 us; the launch traced here: 11 us
  Pallas kernels  10.3 us (93%)
  local copies, waits for them, and re-layouts  0.69 us (6%)
    pallas_call x1, Pallas kernels, body(): pl.pallas_call(kernel, out_shape=pltpu.VMEM(populations.shape, population...  10.3 us
    unnamed x1, local copies, waits for them, and re-layouts  0.69 us

profile of v3, /device:TPU:0, one launch (start us, length us, event | category | flops | bytes accessed | tf_op | source)
XLA Modules:
  0.0 11.0 jit_solution(14887735079160594020)
XLA Ops:
  0.0 10.3 %shard_map.28 = f32[39,3,4,128]{3,2,1,0:T(4,128)S(1)} custom-call(f32[39,3,4,128]{3,2,1,0:T(4,128)} %pop_hbm.1, s32[3,4,128]{2,1,0:T(4,128)} %mask_hbm.1), custom_call_target="tpu_custom_call" | custom-call | tf_op jit(solution)/shard_map/pallas_call | solution.py:320
  10.3 0.7 %copy.4 = f32[39,3,4,128]{3,2,1,0:T(4,128)} copy(f32[39,3,4,128]{3,2,1,0:T(4,128)S(1)} %shard_map.28) | data formatting | bytes 479232

commit v4 on v3

--- a/solution.py
+++ b/solution.py
@@ -99,7 +99,8 @@
             if part3[abc] is not None:
                 third[abc] = accumulate(third[abc], w, part3[abc])
 
-    u = [first[a] / density for a in range(3)]
+    inverse = 1.0 / density
+    u = [first[a] * inverse for a in range(3)]
     relax = 1.0 - 1.0 / relax_time
     const = density
     linear = [first[a] * (1.0 / sound_sq) for a in range(3)]
@@ -148,8 +149,8 @@
     return (-speed, extent), (0, extent + speed), (0, -speed), (extent + speed, extent)
 
 
-def merge_key(speed, extent):
-    return abs(speed) if 2 * abs(speed) <= extent else speed
+def merge_key(speed, rows, extent):
+    return abs(speed) if 2 * rows <= extent else speed
 
 
 def make_plan(nx, ny):
@@ -171,8 +172,8 @@
                         oy,
                         oz,
                         cx,
-                        merge_key(cy, ny) if oy else (cy,),
-                        abs(cz) if oz else (cz,),
+                        merge_key(cy, abs(cy) if oy else ny - abs(cy), ny),
+                        abs(cz) if oz else cz,
                     )
                     if key not in slots:
                         slots[key] = sizes.get((dx, oy, oz), 0)
@@ -193,6 +194,12 @@
     send = dict(zip(names, scratch[: len(names)]))
     recv = dict(zip(messages, scratch[len(names) : len(names) + len(messages)]))
     send_sem, recv_sem, ready = scratch[len(names) + len(messages) :]
+    loads = [
+        pltpu.make_async_copy(pop_hbm, pop_ref, load_sem.at[0]),
+        pltpu.make_async_copy(mask_hbm, mask_ref, load_sem.at[1]),
+    ]
+    for load in loads:
+        load.start()
     here = [lax.axis_index(axis) for axis in ("gx", "gy", "gz")]
 
     def target(step):
@@ -207,12 +214,6 @@
         if step[0] <= 0:
             pl.semaphore_signal(barrier, inc=1, device_id=target(step), device_id_type=MESH)
 
-    loads = [
-        pltpu.make_async_copy(pop_hbm, pop_ref, load_sem.at[0]),
-        pltpu.make_async_copy(mask_hbm, mask_ref, load_sem.at[1]),
-    ]
-    for load in loads:
-        load.start()
     for load in loads:
         load.wait()
 
@@ -240,8 +241,10 @@
             pl.semaphore_wait(barrier, len(messages) - above)
             for step in messages:
                 if step[0] > 0:
+                    copies[step].start()
+            for step in messages:
+                if step[0] > 0:
                     pl.semaphore_signal(ready, inc=1, device_id=target(step), device_id_type=MESH)
-                    copies[step].start()
         cx, cy, cz = speeds[k]
         if cz:
             plane = pltpu.roll(plane, cz % nz, 2)
@@ -278,7 +281,7 @@
     def came_by(step, speed):
         return step == 0 or step * speed > 0
 
-    for step in reversed(messages):
+    for step in sorted(messages, key=lambda step: (0, -1, 1).index(step[0])):
         copies[step].wait_recv()
         got = recv[step]
         dx, sy, sz = step
@@ -291,7 +294,7 @@
                 continue
             _, y_land, _, y_wrap = cut(cy, ny)
             rows = y_wrap if sy else y_land
-            lanes = cut(cz, nz)[3] if sz else every_lane
+            lanes = cut(cz, nz)[3 if sz else 1]
             for source, land, piece_dx, where in pieces[k]:
                 if piece_dx != dx:
                     continue
@@ -307,10 +310,10 @@
     sizes, pieces = make_plan(nx, ny)
     names = sorted(sizes)
     messages = []
-    for dx, oy, oz in [(dx, oy, oz) for oz in (1, 0) for oy in (1, 0) for dx in (1, -1)] + [
-        (0, 1, 1),
+    for dx, oy, oz in [(dx, oy, oz) for dx in (1, -1) for oz in (1, 0) for oy in (1, 0)] + [
         (0, 0, 1),
         (0, 1, 0),
+        (0, 1, 1),
     ]:
         for sy in neighbours(counts[1]) if oy else (0,):
             for sz in neighbours(counts[2]) if oz else (0,):

time: 11.1 us -> 11.1 us (level)
  no operation moved by 1% of the time
where the time goes in v4:
time: 11.1 us; the launch traced here: 10.9 us
  Pallas kernels  10.2 us (92%)
  local copies, waits for them, and re-layouts  0.69 us (6%)
    pallas_call x1, Pallas kernels, body(): pl.pallas_call(kernel, out_shape=pltpu.VMEM(populations.shape, population...  10.2 us
    unnamed x1, local copies, waits for them, and re-layouts  0.69 us

profile of v4, /device:TPU:0, one launch (start us, length us, event | category | flops | bytes accessed | tf_op | source)
XLA Modules:
  0.0 10.9 jit_solution(12659123978048375255)
XLA Ops:
  0.0 10.2 %shard_map.28 = f32[39,3,4,128]{3,2,1,0:T(4,128)S(1)} custom-call(f32[39,3,4,128]{3,2,1,0:T(4,128)} %pop_hbm.1, s32[3,4,128]{2,1,0:T(4,128)} %mask_hbm.1), custom_call_target="tpu_custom_call" | custom-call | tf_op jit(solution)/shard_map/pallas_call | solution.py:323
  10.3 0.7 %copy.4 = f32[39,3,4,128]{3,2,1,0:T(4,128)} copy(f32[39,3,4,128]{3,2,1,0:T(4,128)S(1)} %shard_map.28) | data formatting | bytes 479232

commit v5 on v4

--- a/solution.py
+++ b/solution.py
@@ -193,7 +193,7 @@
     *scratch, pop_ref, mask_ref, load_sem = scratch
     send = dict(zip(names, scratch[: len(names)]))
     recv = dict(zip(messages, scratch[len(names) : len(names) + len(messages)]))
-    send_sem, recv_sem, ready = scratch[len(names) + len(messages) :]
+    send_sem, recv_sem = scratch[len(names) + len(messages) :]
     loads = [
         pltpu.make_async_copy(pop_hbm, pop_ref, load_sem.at[0]),
         pltpu.make_async_copy(mask_hbm, mask_ref, load_sem.at[1]),
@@ -211,8 +211,7 @@
 
     barrier = pltpu.get_barrier_semaphore()
     for step in messages:
-        if step[0] <= 0:
-            pl.semaphore_signal(barrier, inc=1, device_id=target(step), device_id_type=MESH)
+        pl.semaphore_signal(barrier, inc=1, device_id=target(step), device_id_type=MESH)
 
     for load in loads:
         load.wait()
@@ -231,20 +230,16 @@
             device_id=target(step),
             device_id_type=MESH,
         )
-    above = sum(step[0] > 0 for step in messages)
 
     pore = mask_ref[...] == 1
     every_lane = (0, nz)
     moving = sum(speed[0] != 0 for speed in speeds)
     for done, (k, plane) in enumerate(collide(lambda j: pop_ref[j], pore)):
         if done == moving:
-            pl.semaphore_wait(barrier, len(messages) - above)
+            pl.semaphore_wait(barrier, len(messages))
             for step in messages:
-                if step[0] > 0:
+                if step[0]:
                     copies[step].start()
-            for step in messages:
-                if step[0] > 0:
-                    pl.semaphore_signal(ready, inc=1, device_id=target(step), device_id_type=MESH)
         cx, cy, cz = speeds[k]
         if cz:
             plane = pltpu.roll(plane, cz % nz, 2)
@@ -273,10 +268,6 @@
     for step in messages:
         if step[0] == 0:
             copies[step].start()
-    pl.semaphore_wait(ready, above)
-    for step in messages:
-        if step[0] < 0:
-            copies[step].start()
 
     def came_by(step, speed):
         return step == 0 or step * speed > 0
@@ -328,7 +319,6 @@
         scratch_shapes=[shape(name) for name in names]
         + [shape(step) for step in messages]
         + [pltpu.SemaphoreType.DMA((len(messages),)), pltpu.SemaphoreType.DMA((len(messages),))]
-        + [pltpu.SemaphoreType.REGULAR]
         + [
             pltpu.VMEM(populations.shape, populations.dtype),
             pltpu.VMEM(pore_mask.shape, pore_mask.dtype),

time: 11.1 us -> 11 us (level)
  no operation moved by 1% of the time
where the time goes in v5:
time: 11 us; the launch traced here: 10.9 us
  Pallas kernels  10.2 us (93%)
  local copies, waits for them, and re-layouts  0.69 us (6%)
    pallas_call x1, Pallas kernels, body(): pl.pallas_call(kernel, out_shape=pltpu.VMEM(populations.shape, population...  10.2 us
    unnamed x1, local copies, waits for them, and re-layouts  0.69 us

profile of v5, /device:TPU:0, one launch (start us, length us, event | category | flops | bytes accessed | tf_op | source)
XLA Modules:
  0.0 10.9 jit_solution(7624992569092778823)
XLA Ops:
  0.0 10.2 %shard_map.28 = f32[39,3,4,128]{3,2,1,0:T(4,128)S(1)} custom-call(f32[39,3,4,128]{3,2,1,0:T(4,128)} %pop_hbm.1, s32[3,4,128]{2,1,0:T(4,128)} %mask_hbm.1), custom_call_target="tpu_custom_call" | custom-call | tf_op jit(solution)/shard_map/pallas_call | solution.py:314
  10.2 0.7 %copy.4 = f32[39,3,4,128]{3,2,1,0:T(4,128)} copy(f32[39,3,4,128]{3,2,1,0:T(4,128)S(1)} %shard_map.28) | data formatting | bytes 479232
